TPU v7x, 32 devices: a whole 2x2x4 slice. The times are simulated.
32 devices in a mesh: groups: 2 (over y), fsdp: 4 (over z), rep: 4 (over x, core).
Axes of the slice: x: 2, y: 2, z: 4, core: 2. Of those that a mesh axis runs over, the one named last changes fastest.
Arguments:
- images: bfloat16 [8, 16, 256, 320], P(('groups', 'rep'), 'fsdp'), parts along dimension 0, may hold values from -60 to 60
- gains: float32 [2, 320], replicated, may hold values from 0.5 to 1.5
- conv_weight: bfloat16 [2880, 320], P('fsdp'), may hold values from -0.109375 to 0.109375
- cotangent: bfloat16 [8, 8, 128, 320], P(('groups', 'rep'), 'fsdp'), parts along dimension 0, may hold values from -60 to 60
Outputs:
- output_maps: bfloat16 [8, 8, 128, 320], P(('groups', 'rep'), 'fsdp'), parts along dimension 0
- input_grad: bfloat16 [8, 16, 256, 320], P(('groups', 'rep'), 'fsdp'), parts along dimension 0
- weight_grad: float32 [5760, 320], P(('groups', 'fsdp')), parts along dimension 0
- gain_grad: float32 [4, 320], P('groups'), parts along dimension 0
There are 2 independent parts, one for each index of `groups`. A program takes and returns all parts, laid end to end along the dimension named above; an argument that names none is the same for every part. Nothing has to cross between parts.
All inputs are finite; a program needn't handle non-finite values.
Results may differ from a plain program's by a relative error of at most 0.0095.
Values may be sent and summed in bfloat16 or wider, within the bound.
A program may use at most 64 MiB of HBM per device.

v0:
```python
import jax
import jax.numpy as jnp
from jax import lax
from jax.sharding import PartitionSpec as P

GROUPS = 32


def passed_along(shard, axis, by):
    size = lax.axis_size(axis)
    pairs = [(i, i + by) for i in range(size) if 0 <= i + by < size]
    return lax.ppermute(shard, axis, pairs)


def spread_taps(first, middle, last, axis):
    length = first.shape[axis]
    widths_end = [(0, 0)] * first.ndim
    widths_end[axis] = (0, 1)
    widths_start = [(0, 0)] * first.ndim
    widths_start[axis] = (1, 0)
    even = jnp.pad(first, widths_end) + jnp.pad(last, widths_start)
    odd = jnp.pad(middle, widths_end)
    merged = jnp.stack([even, odd], axis=axis + 1)
    shape = list(even.shape)
    shape[axis] = 2 * (length + 1)
    merged = merged.reshape(shape)
    return lax.slice_in_dim(merged, 0, 2 * length + 1, axis=axis)


def shards(images, gains, conv_weight, cotangent):
    batch, rows, width, chans = images.shape
    outs_ch = conv_weight.shape[1]
    n_fsdp = lax.axis_size("fsdp")
    per_group = chans // GROUPS
    x_val = images.astype(jnp.float32)
    grouped = x_val.reshape(batch, rows, width, GROUPS, per_group)
    part_one = jnp.sum(grouped, axis=(1, 2, 4))
    part_two = jnp.sum(grouped * grouped, axis=(1, 2, 4))
    full_weight = lax.all_gather(conv_weight, "fsdp", axis=0, tiled=True)
    sum_one, sum_two = lax.psum((part_one, part_two), "fsdp")
    count = rows * n_fsdp * width * per_group
    mean = sum_one / count
    rstd = 1.0 / jnp.sqrt(sum_two / count - mean * mean + 1e-05)
    normed_g = (grouped - mean[:, None, None, :, None]) * rstd[:, None, None, :, None]
    normed = normed_g.reshape(x_val.shape)
    z_val = gains[0] * normed + gains[1]
    act = (z_val * jax.nn.sigmoid(z_val)).astype(jnp.bfloat16)
    above = passed_along(act[:, rows - 1 : rows], "fsdp", 1)
    padded = jnp.concatenate([above, act], axis=1)
    kernel = full_weight.reshape(3, 3, chans, outs_ch)
    result = lax.conv_general_dilated(
        padded,
        kernel,
        (2, 2),
        ((0, 0), (1, 0)),
        dimension_numbers=("NHWC", "HWIO", "NHWC"),
        preferred_element_type=jnp.float32,
    )
    output_maps = result.astype(jnp.bfloat16)
    patch_grad = jnp.einsum(
        "bijo,ko->bijk", cotangent, full_weight, preferred_element_type=jnp.float32
    )
    half_rows, half_cols = (cotangent.shape[1], cotangent.shape[2])
    taps = patch_grad.reshape(batch, half_rows, half_cols, 3, 3, chans)
    by_row = [
        spread_taps(
            taps[:, :, :, row_tap, 0], taps[:, :, :, row_tap, 1], taps[:, :, :, row_tap, 2], 2
        )
        for row_tap in range(3)
    ]
    grid = spread_taps(by_row[0], by_row[1], by_row[2], 1)[:, :, 1:]
    from_below = passed_along(grid[:, 0:1].astype(jnp.bfloat16), "fsdp", -1).astype(jnp.float32)
    filler = jnp.zeros((batch, rows - 1, width, chans), jnp.float32)
    act_grad = grid[:, 1:] + jnp.concatenate([filler, from_below], axis=1)
    padded_cols = jnp.pad(padded, ((0, 0), (0, 0), (1, 0), (0, 0)))
    blocks = []
    for row_tap in range(3):
        for col_tap in range(3):
            window = padded_cols[:, row_tap : row_tap + rows : 2, col_tap : col_tap + width : 2]
            blocks.append(
                jnp.einsum("bijc,bijo->co", window, cotangent, preferred_element_type=jnp.float32)
            )
    total_pixels = batch * lax.axis_size("rep") * half_rows * n_fsdp * half_cols
    scale = 1.0 / jnp.sqrt(jnp.float32(total_pixels))
    weight_term = jnp.concatenate(blocks, axis=0) * scale
    sig = jax.nn.sigmoid(z_val)
    z_grad = act_grad * sig * (1.0 + z_val * (1.0 - sig))
    u_part = jnp.sum(z_grad * normed, axis=(1, 2))
    v_part = jnp.sum(z_grad, axis=(1, 2))
    u_sum, v_sum = lax.psum((u_part, v_part), "fsdp")
    gain_term = jnp.stack([jnp.sum(u_sum, axis=0), jnp.sum(v_sum, axis=0)]) * scale
    su_val = jnp.sum((gains[0] * u_sum).reshape(batch, GROUPS, per_group), axis=-1)
    sv_val = jnp.sum((gains[0] * v_sum).reshape(batch, GROUPS, per_group), axis=-1)
    scaled = (gains[0] * z_grad).reshape(grouped.shape)
    dx_val = rstd[:, None, None, :, None] * (
        scaled
        - sv_val[:, None, None, :, None] / count
        - normed_g * su_val[:, None, None, :, None] / count
    )
    input_grad = dx_val.reshape(x_val.shape).astype(jnp.bfloat16)
    owned = lax.psum_scatter(weight_term, "fsdp", scatter_dimension=0, tiled=True)
    weight_grad, gain_grad = (
        lax.psum(owned.astype(jnp.bfloat16), "rep").astype(jnp.float32),
        lax.psum(gain_term.astype(jnp.bfloat16), "rep").astype(jnp.float32),
    )
    return (output_maps, input_grad, weight_grad, gain_grad)


def solution(mesh):
    in_specs = (
        P(("groups", "rep"), "fsdp", None, None),
        P(),
        P("fsdp", None),
        P(("groups", "rep"), "fsdp", None, None),
    )
    out_specs = (
        P(("groups", "rep"), "fsdp", None, None),
        P(("groups", "rep"), "fsdp", None, None),
        P(("groups", "fsdp"), None),
        P("groups", None),
    )
    return jax.shard_map(shards, mesh=mesh, in_specs=in_specs, out_specs=out_specs, check_vma=False)
```

profile of v0, /device:TPU:0, one launch (start us, length us, event | category | flops | bytes accessed | tf_op | source)
XLA Modules:
  0.0 300.0 jit_solution(18185248881887564390)
XLA Ops:
  8.0 1.4 convert_reduce_fusion
  9.8 13.6 %all-reduce.15 = (f32[1,32]{1,0:T(1,128)S(1)}, f32[1,32]{1,0:T(1,128)S(1)}) all-reduce(f32[1,32]{1,0:T(1,128)S(1)} %bitcast.156, f32[1,32]{1,0:T(1,128)S(1)} %bitcast.157), channel_id=1, replica_groups=mesh['groups'=2,'fsdp'=4,'rep'=4] {'fsdp'}, use_global_device_ids=true, to_apply=%region_5.6 | all-reduce | flops 64 | bytes 512 | tf_op jit(solution)/shard_map/psum | solution.py:40
  23.3 32.5 %all-gather.3.cloned.1.call-done = bf16[4,720,320]{1,2,0:T(8,128)(2,1)} async-done(((bf16[1,720,320]{1,2,0:T(8,128)(2,1)}), bf16[4,720,320]{1,2,0:T(8,128)(2,1)}) %all-gather.3.cloned.1.call-update) | async-done | bytes 1843216 | tf_op jit(solution)/shard_map/all_gather | solution.py:39
  55.9 3.0 %copy.34 = bf16[4,720,320]{2,1,0:T(8,128)(2,1)S(1)} copy(bf16[4,720,320]{1,2,0:T(8,128)(2,1)} %all-gather.3.cloned.1.call-done) | data formatting | bytes 3686400 | tf_op jit(solution)/shard_map/all_gather | solution.py:39
  62.7 1.4 pad_bitcast_fusion
  69.7 3.8 %copy.45 = f32[1,3,2,257,320]{3,4,2,1,0:T(8,128)} copy(f32[1,3,2,257,320]{4,1,3,2,0:T(4,128)S(1)} %pad_maximum_fusion) | data formatting | bytes 3947520 | tf_op jit(solution)/shard_map/stack | solution.py:23
  74.7 1.3 collective-permute-start.1
  76.4 6.1 %collective-permute-done.1 = bf16[1,1,256,320]{2,3,1,0:T(8,128)(2,1)S(1)} collective-permute-done((bf16[1,1,256,320]{2,3,1,0:T(8,128)(2,1)S(1)}, bf16[1,1,256,320]{2,3,1,0:T(8,128)(2,1)S(1)}, u32[]{:S(2)}, u32[]{:S(2)}) %collective-permute-start.1) | collective-permute-done | bytes 163872 | tf_op jit(solution)/shard_map/ppermute | solution.py:12
  82.5 2.8 fusion.54
  85.4 2.2 collective-permute-start
  87.6 2.6 collective-permute-done
  90.8 6.4 %slice.104 = bf16[1,2,128,320]{2,3,1,0:T(8,128)(2,1)} slice(bf16[1,5,257,320]{2,3,1,0:T(8,128)(2,1)S(1)} %pad.58), slice={[0:1:1], [0:4:2], [0:256:2], [0:320:1]} | slice | bytes 327680 | tf_op jit(solution)/shard_map/slice | solution.py:79
  97.2 6.4 %slice.105 = bf16[1,2,128,320]{2,3,1,0:T(8,128)(2,1)} slice(bf16[1,5,257,320]{2,3,1,0:T(8,128)(2,1)S(1)} %pad.58), slice={[0:1:1], [0:4:2], [1:257:2], [0:320:1]} | slice | bytes 327680 | tf_op jit(solution)/shard_map/slice | solution.py:79
  103.6 6.4 %slice.106 = bf16[1,2,128,320]{2,3,1,0:T(8,128)(2,1)} slice(bf16[1,5,257,320]{2,3,1,0:T(8,128)(2,1)S(1)} %pad.58), slice={[0:1:1], [0:4:2], [2:257:2], [0:320:1]} | slice | bytes 327680 | tf_op jit(solution)/shard_map/slice | solution.py:79
  110.1 6.4 %slice.107 = bf16[1,2,128,320]{2,3,1,0:T(8,128)(2,1)} slice(bf16[1,5,257,320]{2,3,1,0:T(8,128)(2,1)S(1)} %pad.58), slice={[0:1:1], [1:5:2], [0:256:2], [0:320:1]} | slice | bytes 327680 | tf_op jit(solution)/shard_map/slice | solution.py:79
  116.4 6.4 %slice.108 = bf16[1,2,128,320]{2,3,1,0:T(8,128)(2,1)} slice(bf16[1,5,257,320]{2,3,1,0:T(8,128)(2,1)S(1)} %pad.58), slice={[0:1:1], [1:5:2], [1:257:2], [0:320:1]} | slice | bytes 327680 | tf_op jit(solution)/shard_map/slice | solution.py:79
  122.8 6.4 %slice.109 = bf16[1,2,128,320]{2,3,1,0:T(8,128)(2,1)} slice(bf16[1,5,257,320]{2,3,1,0:T(8,128)(2,1)S(1)} %pad.58), slice={[0:1:1], [1:5:2], [2:257:2], [0:320:1]} | slice | bytes 327680 | tf_op jit(solution)/shard_map/slice | solution.py:79
  129.3 6.4 %slice.110 = bf16[1,2,128,320]{2,3,1,0:T(8,128)(2,1)} slice(bf16[1,5,257,320]{2,3,1,0:T(8,128)(2,1)S(1)} %pad.58), slice={[0:1:1], [2:5:2], [0:256:2], [0:320:1]} | slice | bytes 327680 | tf_op jit(solution)/shard_map/slice | solution.py:79
  135.7 6.4 %slice.111 = bf16[1,2,128,320]{2,3,1,0:T(8,128)(2,1)} slice(bf16[1,5,257,320]{2,3,1,0:T(8,128)(2,1)S(1)} %pad.58), slice={[0:1:1], [2:5:2], [1:257:2], [0:320:1]} | slice | bytes 327680 | tf_op jit(solution)/shard_map/slice | solution.py:79
  142.1 6.5 %slice.112 = bf16[1,2,128,320]{2,3,1,0:T(8,128)(2,1)} slice(bf16[1,5,257,320]{2,3,1,0:T(8,128)(2,1)S(1)} %pad.58), slice={[0:1:1], [2:5:2], [2:257:2], [0:320:1]} | slice | bytes 327680 | tf_op jit(solution)/shard_map/slice | solution.py:79
  148.6 1.2 convolution_bitcast_fusion.9
  158.5 4.8 %concatenate.14 = f32[2880,320]{0,1:T(8,128)} concatenate(f32[320,320]{0,1:T(8,128)S(1)} %convolution_bitcast_fusion.9, f32[320,320]{0,1:T(8,128)S(1)} %convolution_bitcast_fusion.8, f32[320,320]{0,1:T(8,128)} %convolution_bitcast_fusion.7, f32[320,320]{0,1:T(8,128)} %convolution_bitcast_fusion.6, f32[320,320]{0,1:T(8,128)} %convolution_bitcast_fusion.5, ...), dimensions={0} | concatenate | bytes 7372800 | tf_op jit(solution)/shard_map/concatenate | solution.py:85
  163.3 4.1 %broadcast_multiply_fusion = f32[2880,320]{0,1:T(8,128)} fusion(f32[2880,320]{0,1:T(8,128)} %concatenate.14), kind=kLoop, calls=%fused_computation.6 | loop fusion | flops 921600 | bytes 7372800 | tf_op jit(solution)/shard_map/mul | solution.py:85
  167.4 5.4 %copy.48 = f32[2880,320]{1,0:T(8,128)} copy(f32[2880,320]{0,1:T(8,128)} %broadcast_multiply_fusion) | data formatting | bytes 7372800
  172.9 11.8 %all-reduce.14 = (f32[1,320]{1,0:T(1,128)S(1)}, f32[1,320]{1,0:T(1,128)S(1)}) all-reduce(f32[1,320]{1,0:T(1,128)S(1)} %reduce_sum.93, f32[1,320]{1,0:T(1,128)S(1)} %reduce_sum.96), channel_id=1, replica_groups=mesh['groups'=2,'fsdp'=4,'rep'=4] {'fsdp'}, use_global_device_ids=true, to_apply=%region_7.8 | all-reduce | flops 640 | bytes 5120 | tf_op jit(solution)/shard_map/psum | solution.py:90
  185.6 6.1 %psum.47 = bf16[2,320]{1,0:T(2,128)(2,1)S(1)} all-reduce(bf16[2,320]{1,0:T(2,128)(2,1)S(1)} %fusion.49), channel_id=1, replica_groups=mesh['groups'=2,'fsdp'=4,'rep'=4] {'rep'}, use_global_device_ids=true, to_apply=%region_14.15 | all-reduce | flops 640 | bytes 2560 | tf_op jit(solution)/shard_map/psum | solution.py:104
  192.3 1.3 fusion.19
  195.1 1.5 copy-done.2
  197.9 56.9 %reduce-scatter.4.cloned.1.call-done = f32[720,320]{1,0:T(8,128)} async-done(((f32[2880,320]{1,0:T(8,128)}), f32[720,320]{1,0:T(8,128)}) %reduce-scatter.4.cloned.1.call-update) | async-done | bytes 921616
  254.8 2.2 copy.49
  258.1 33.3 %all-reduce.18.cloned.1.call-done = bf16[720,320]{0,1:T(8,128)(2,1)} async-done(((bf16[720,320]{0,1:T(8,128)(2,1)}), bf16[720,320]{0,1:T(8,128)(2,1)}) %all-reduce.18.cloned.1.call-update) | async-done | bytes 460816 | tf_op jit(solution)/shard_map/psum | solution.py:103
  291.4 2.0 convert_element_type.53
  (100 shorter events, 26.4 us)
Async XLA Ops:
  7.2 51.8 %copy-start = (bf16[1,2,128,320]{2,3,1,0:T(8,128)(2,1)S(1)}, bf16[1,2,128,320]{2,3,1,0:T(8,128)(2,1)}, u32[]{:S(2)}) copy-start(bf16[1,2,128,320]{2,3,1,0:T(8,128)(2,1)} %param.7) | copy-start | bytes 491524
  7.2 48.7 %all-gather.3.cloned.1.call-start = ((), (), s32[]{:S(2)}) async-start(), calls=%async_computation.2 | async-start | bytes 2457600 | tf_op jit(solution)/shard_map/all_gather | solution.py:39
  7.9 246.9 %reduce-scatter.4.cloned.1.call-start = ((), (), s32[]{:S(2)}) async-start(), calls=%async_computation.3 | async-start | bytes 5529600
  58.9 1.4 copy-start.1
  62.7 1.5 copy-start.7
  65.2 1.0 copy-start.5
  65.2 1.1 copy-start.6
  67.6 1.4 copy-start.3
  69.7 6.6 %copy-start.15 = (f32[2,320]{1,0:T(2,128)S(1)}, f32[2,320]{1,0:T(2,128)}, u32[]{:S(2)}) copy-start(f32[2,320]{1,0:T(2,128)} %param.5) | copy-start | bytes 7684
  74.7 7.8 %collective-permute-start.1 = (bf16[1,1,256,320]{2,3,1,0:T(8,128)(2,1)S(1)}, bf16[1,1,256,320]{2,3,1,0:T(8,128)(2,1)S(1)}, u32[]{:S(2)}, u32[]{:S(2)}) collective-permute-start(bf16[1,1,256,320]{2,3,1,0:T(8,128)(2,1)S(1)} %slice.152), channel_id=1, source_target_pairs={{4,0},{8,4},{12,8},{5,1},{9,5},{13,9},{6,2},{10,6},{14,10},{7,3},{... | collective-permute-start | bytes 491528 | tf_op jit(solution)/shard_map/ppermute | solution.py:12
  85.4 4.8 %collective-permute-start = (bf16[1,1,256,320]{2,3,1,0:T(8,128)(2,1)S(1)}, bf16[1,1,256,320]{2,3,1,0:T(8,128)(2,1)S(1)}, u32[]{:S(2)}, u32[]{:S(2)}) collective-permute-start(bf16[1,1,256,320]{2,3,1,0:T(8,128)(2,1)S(1)} %slice.115), channel_id=1, source_target_pairs={{0,4},{4,8},{8,12},{1,5},{5,9},{9,13},{2,6},{6,10},{10,14},{3,7},{... | collective-permute-start | bytes 491528 | tf_op jit(solution)/shard_map/ppermute | solution.py:12
  148.6 2.5 copy-start.14
  148.6 3.5 %copy-start.13 = (bf16[1,2,128,320]{2,3,1,0:T(8,128)(2,1)S(1)}, bf16[1,2,128,320]{2,3,1,0:T(8,128)(2,1)}, u32[]{:S(2)}) copy-start(bf16[1,2,128,320]{2,3,1,0:T(8,128)(2,1)} %slice.107) | copy-start | bytes 491524
  149.8 3.4 %copy-start.12 = (bf16[1,2,128,320]{2,3,1,0:T(8,128)(2,1)S(1)}, bf16[1,2,128,320]{2,3,1,0:T(8,128)(2,1)}, u32[]{:S(2)}) copy-start(bf16[1,2,128,320]{2,3,1,0:T(8,128)(2,1)} %slice.108) | copy-start | bytes 491524
  151.1 3.2 %copy-start.11 = (bf16[1,2,128,320]{2,3,1,0:T(8,128)(2,1)S(1)}, bf16[1,2,128,320]{2,3,1,0:T(8,128)(2,1)}, u32[]{:S(2)}) copy-start(bf16[1,2,128,320]{2,3,1,0:T(8,128)(2,1)} %slice.109) | copy-start | bytes 491524
  152.1 3.2 %copy-start.10 = (bf16[1,2,128,320]{2,3,1,0:T(8,128)(2,1)S(1)}, bf16[1,2,128,320]{2,3,1,0:T(8,128)(2,1)}, u32[]{:S(2)}) copy-start(bf16[1,2,128,320]{2,3,1,0:T(8,128)(2,1)} %slice.110) | copy-start | bytes 491524
  153.2 3.2 %copy-start.9 = (bf16[1,2,128,320]{2,3,1,0:T(8,128)(2,1)S(1)}, bf16[1,2,128,320]{2,3,1,0:T(8,128)(2,1)}, u32[]{:S(2)}) copy-start(bf16[1,2,128,320]{2,3,1,0:T(8,128)(2,1)} %slice.111) | copy-start | bytes 491524
  154.2 3.2 %copy-start.8 = (bf16[1,2,128,320]{2,3,1,0:T(8,128)(2,1)S(1)}, bf16[1,2,128,320]{2,3,1,0:T(8,128)(2,1)}, u32[]{:S(2)}) copy-start(bf16[1,2,128,320]{2,3,1,0:T(8,128)(2,1)} %slice.112) | copy-start | bytes 491524
  172.8 19.4 %copy-start.4 = (bf16[1,4,256,320]{2,3,1,0:T(8,128)(2,1)S(1)}, bf16[1,4,256,320]{2,3,1,0:T(8,128)(2,1)}, u32[]{:S(2)}) copy-start(bf16[1,4,256,320]{2,3,1,0:T(8,128)(2,1)} %param.4) | copy-start | bytes 1966084
  172.9 118.5 %all-reduce.18.cloned.1.call-start = ((), (), s32[]{:S(2)}) async-start(), calls=%async_computation.1 | async-start | bytes 983040 | tf_op jit(solution)/shard_map/psum | solution.py:103
  194.9 1.7 copy-start.2
  195.0 1.7 copy-start.16
Sparse Core Ops, SparseCore 0:
  9.6 46.2 all-gather.2
  173.0 81.7 reduce-scatter.3
  257.9 33.4 all-reduce.17
where the time goes:
time: 301 us; the launch traced here: 300 us
  waiting for transfers between devices  132 us (44%)
  local copies, waits for them, and re-layouts  91.5 us (30%)
  blocking collectives  31.4 us (10%)
  other arithmetic  15.2 us (5%)
  between operations  14.2 us (5%)
  matrix products  11.8 us (4%)
  starting transfers between devices  3.59 us (1%)
    slice x9, local copies, waits for them, and re-layouts, shards(): window = padded_cols[:, row_tap:row_tap + rows:2, col_tap:col_tap + width:2]  57.8 us
    unnamed x4, waiting for transfers between devices  57.6 us
    psum x1, waiting for transfers between devices, shards(): lax.psum(owned.astype(jnp.bfloat16), 'rep').astype(jnp.float32)  33.3 us
    all_gather x1, waiting for transfers between devices, shards(): full_weight = lax.all_gather(conv_weight, 'fsdp', axis=0, tiled=True)  32.5 us
    psum x1, blocking collectives, shards(): sum_one, sum_two = lax.psum((part_one, part_two), 'fsdp')  13.6 us
    unnamed x38, local copies, waits for them, and re-layouts  12.8 us
    psum x1, blocking collectives, shards(): u_sum, v_sum = lax.psum((u_part, v_part), 'fsdp')  11.8 us
    dot_general x9, matrix products, shards(): jnp.einsum('bijc,bijo->co', window, cotangent, preferred_element_type=jnp...  9.83 us
  transfers between devices with their start and end apart: 5, of which 5 were waited for; matrix products, arithmetic and copies ran while one was open for 3% of the time, Pallas kernels for 0%

commit v1 on v0

--- a/solution.py
+++ b/solution.py
@@ -36,7 +36,12 @@
     grouped = x_val.reshape(batch, rows, width, GROUPS, per_group)
     part_one = jnp.sum(grouped, axis=(1, 2, 4))
     part_two = jnp.sum(grouped * grouped, axis=(1, 2, 4))
-    full_weight = lax.all_gather(conv_weight, "fsdp", axis=0, tiled=True)
+    ring = [conv_weight]
+    for hop in range(3):
+        ring.append(lax.ppermute(ring[-1], "fsdp", [(dev, (dev + 1) % 4) for dev in range(4)]))
+    full_weight = jnp.roll(
+        jnp.concatenate(ring[::-1], axis=0), (lax.axis_index("fsdp") + 1) * ring[0].shape[0], axis=0
+    )
     sum_one, sum_two = lax.psum((part_one, part_two), "fsdp")
     count = rows * n_fsdp * width * per_group
     mean = sum_one / count

time: 301 us -> 316 us (1.050)
  local copies, waits for them, and re-layouts: 91.5 us -> 105 us
  waiting for transfers between devices: 132 us -> 121 us
  other arithmetic: 15.2 us -> 22.5 us
  starting transfers between devices: 3.59 us -> 8.33 us
    all_gather x1 -> x0, waiting for transfers between devices: 32.5 us -> none  [shards(): full_weight = lax.all_gather(conv_weight, 'fsdp', axis=0, tiled=True)]
    ppermute x0 -> x3, waiting for transfers between devices: none -> 27.7 us  [shards(): lax.ppermute(ring[-1], 'fsdp', [(dev, (dev + 1) % 4) for dev in range(4)])]
    concatenate x0 -> x1, local copies, waits for them, and re-layouts: none -> 6.69 us  [shards(): jnp.roll(jnp.concatenate(ring[::-1], axis=0), (lax.axis_index('fsdp') + 1...]
    unnamed x38 -> x49, local copies, waits for them, and re-layouts: 12.8 us -> 18.6 us
    unnamed x4 -> x3, waiting for transfers between devices: 57.6 us -> 52.2 us
    dynamic_slice x0 -> x2, local copies, waits for them, and re-layouts: none -> 4.99 us  [shards(): jnp.roll(jnp.concatenate(ring[::-1], axis=0), (lax.axis_index('fsdp') + 1...]
    another operation x8, other arithmetic: 2.36 us -> 6.49 us  [spread_taps(): merged = jnp.stack([even, odd], axis=axis + 1)]
    another operation x5 -> x2, local copies, waits for them, and re-layouts: 7.35 us -> 7.25 us  [spread_taps(): merged = jnp.stack([even, odd], axis=axis + 1)]
  transfers between devices with their start and end apart: 5 -> 7, of which waited for: 5 -> 6; matrix products, arithmetic and copies ran while one was open for 3% -> 4% of each run, Pallas kernels for 0% -> 0%
where the time goes in v1:
time: 316 us; the launch traced here: 314 us
  waiting for transfers between devices  121 us (38%)
  local copies, waits for them, and re-layouts  105 us (33%)
  blocking collectives  31.2 us (10%)
  other arithmetic  22.5 us (7%)
  between operations  14.5 us (5%)
  matrix products  11.1 us (4%)
  starting transfers between devices  8.33 us (3%)
    slice x9, local copies, waits for them, and re-layouts, shards(): window = padded_cols[:, row_tap:row_tap + rows:2, col_tap:col_tap + width:2]  57.2 us
    unnamed x3, waiting for transfers between devices  52.2 us
    psum x1, waiting for transfers between devices, shards(): lax.psum(owned.astype(jnp.bfloat16), 'rep').astype(jnp.float32)  33.2 us
    ppermute x3, waiting for transfers between devices, shards(): lax.ppermute(ring[-1], 'fsdp', [(dev, (dev + 1) % 4) for dev in range(4)])  27.7 us
    unnamed x49, local copies, waits for them, and re-layouts  18.6 us
    psum x1, blocking collectives, shards(): sum_one, sum_two = lax.psum((part_one, part_two), 'fsdp')  14 us
    psum x1, blocking collectives, shards(): u_sum, v_sum = lax.psum((u_part, v_part), 'fsdp')  11.1 us
    dot_general x9, matrix products, shards(): jnp.einsum('bijc,bijo->co', window, cotangent, preferred_element_type=jnp...  9.05 us
  transfers between devices with their start and end apart: 7, of which 6 were waited for; matrix products, arithmetic and copies ran while one was open for 4% of the time, Pallas kernels for 0%

profile of v1, /device:TPU:0, one launch (start us, length us, event | category | flops | bytes accessed | tf_op | source)
XLA Modules:
  0.0 314.3 jit_solution(13266707511976684086)
XLA Ops:
  7.2 3.1 collective-permute-start.1
  10.3 13.5 %collective-permute-done.1 = bf16[720,320]{0,1:T(8,128)(2,1)S(1)} collective-permute-done((bf16[720,320]{0,1:T(8,128)(2,1)}, bf16[720,320]{0,1:T(8,128)(2,1)S(1)}, u32[]{:S(2)}, u32[]{:S(2)}) %collective-permute-start.1) | collective-permute-done | bytes 460832 | tf_op jit(solution)/shard_map/ppermute | solution.py:41
  23.8 14.2 %collective-permute-done.2 = bf16[720,320]{0,1:T(8,128)(2,1)S(1)} collective-permute-done((bf16[720,320]{0,1:T(8,128)(2,1)S(1)}, bf16[720,320]{0,1:T(8,128)(2,1)S(1)}, u32[]{:S(2)}, u32[]{:S(2)}) %collective-permute-start.2) | collective-permute-done | bytes 460832 | tf_op jit(solution)/shard_map/ppermute | solution.py:41
  39.8 14.0 %all-reduce.15 = (f32[1,32]{1,0:T(1,128)}, f32[1,32]{1,0:T(1,128)}) all-reduce(f32[1,32]{1,0:T(1,128)S(1)} %bitcast.139, f32[1,32]{1,0:T(1,128)S(1)} %bitcast.140), channel_id=1, replica_groups=mesh['groups'=2,'fsdp'=4,'rep'=4] {'fsdp'}, use_global_device_ids=true, to_apply=%region_5.6 | all-reduce | flops 64 | bytes 512 | tf_op jit(solution)/shard_map/psum | solution.py:45
  53.8 6.7 %concatenate.18 = bf16[5760,320]{0,1:T(8,128)(2,1)} concatenate(bf16[720,320]{0,1:T(8,128)(2,1)S(1)} %collective-permute-done.3, bf16[720,320]{0,1:T(8,128)(2,1)S(1)} %collective-permute-done.2, bf16[720,320]{0,1:T(8,128)(2,1)S(1)} %collective-permute-done.1, bf16[720,320]{0,1:T(8,128)(2,1)} %param.6, bf16[720,320]{0,1:T(8,128)(2,1)S(1)} %collective-permute-done.3, ...), dimensions={0} | concatenate | bytes 7372800 | tf_op jit(solution)/shard_map/jit(_roll_dynamic)/concatenate | solution.py:42
  60.5 2.4 constant_dynamic-slice_fusion
  79.6 2.4 pad_maximum_fusion
  82.0 5.8 %copy.45 = f32[1,3,2,257,320]{3,4,2,1,0:T(8,128)} copy(f32[1,3,2,257,320]{4,1,3,2,0:T(4,128)} %pad_maximum_fusion) | data formatting | bytes 3947520 | tf_op jit(solution)/shard_map/stack | solution.py:23
  90.7 5.5 %collective-permute-done.4 = bf16[1,1,256,320]{2,3,1,0:T(8,128)(2,1)S(1)} collective-permute-done((bf16[1,1,256,320]{2,3,1,0:T(8,128)(2,1)S(1)}, bf16[1,1,256,320]{2,3,1,0:T(8,128)(2,1)S(1)}, u32[]{:S(2)}, u32[]{:S(2)}) %collective-permute-start.4) | collective-permute-done | bytes 163872 | tf_op jit(solution)/shard_map/ppermute | solution.py:12
  96.2 3.7 %fusion.56 = (f32[320]{0:T(512)S(1)}, f32[320]{0:T(512)S(1)}, f32[1,4,256,320]{2,3,1,0:T(8,128)}, bf16[1,4,256,320]{2,3,1,0:T(8,128)(2,1)S(1)}) fusion(f32[320]{0:T(512)S(1)} %mul.125, f32[320]{0:T(512)S(1)} %sub.61, bf16[1,4,256,320]{2,3,1,0:T(8,128)(2,1)S(1)} %copy-done.2, f32[320]{0:T(512)S(1)} %get-tuple-element.19, f32[320]{0:T(512)S(1)} %get-tuple-element.18, ...), kind=kLoop, calls=%fused_computation.95 | loop fusion | flops 6552960 | bytes 4103680 | tf_op jit(solution)/shard_map/reduce_sum | solution.py:94
  99.8 3.9 %collective-permute-start = (bf16[1,1,256,320]{2,3,1,0:T(8,128)(2,1)S(1)}, bf16[1,1,256,320]{2,3,1,0:T(8,128)(2,1)S(1)}, u32[]{:S(2)}, u32[]{:S(2)}) collective-permute-start(bf16[1,1,256,320]{2,3,1,0:T(8,128)(2,1)S(1)} %slice.115), channel_id=1, source_target_pairs={{0,4},{4,8},{8,12},{1,5},{5,9},{9,13},{2,6},{6,10},{10,14},{3,7},{... | collective-permute-start | bytes 491528 | tf_op jit(solution)/shard_map/ppermute | solution.py:12
  103.7 2.6 collective-permute-done
  107.9 6.4 %slice.104 = bf16[1,2,128,320]{2,3,1,0:T(8,128)(2,1)} slice(bf16[1,5,257,320]{2,3,1,0:T(8,128)(2,1)S(1)} %pad.58), slice={[0:1:1], [0:4:2], [0:256:2], [0:320:1]} | slice | bytes 327680 | tf_op jit(solution)/shard_map/slice | solution.py:84
  114.3 5.8 %slice.105 = bf16[1,2,128,320]{2,3,1,0:T(8,128)(2,1)S(1)} slice(bf16[1,5,257,320]{2,3,1,0:T(8,128)(2,1)S(1)} %pad.58), slice={[0:1:1], [0:4:2], [1:257:2], [0:320:1]} | slice | bytes 327680 | tf_op jit(solution)/shard_map/slice | solution.py:84
  120.1 6.5 %slice.106 = bf16[1,2,128,320]{2,3,1,0:T(8,128)(2,1)} slice(bf16[1,5,257,320]{2,3,1,0:T(8,128)(2,1)S(1)} %pad.58), slice={[0:1:1], [0:4:2], [2:257:2], [0:320:1]} | slice | bytes 327680 | tf_op jit(solution)/shard_map/slice | solution.py:84
  126.5 6.4 %slice.107 = bf16[1,2,128,320]{2,3,1,0:T(8,128)(2,1)} slice(bf16[1,5,257,320]{2,3,1,0:T(8,128)(2,1)S(1)} %pad.58), slice={[0:1:1], [1:5:2], [0:256:2], [0:320:1]} | slice | bytes 327680 | tf_op jit(solution)/shard_map/slice | solution.py:84
  132.9 6.4 %slice.108 = bf16[1,2,128,320]{2,3,1,0:T(8,128)(2,1)} slice(bf16[1,5,257,320]{2,3,1,0:T(8,128)(2,1)S(1)} %pad.58), slice={[0:1:1], [1:5:2], [1:257:2], [0:320:1]} | slice | bytes 327680 | tf_op jit(solution)/shard_map/slice | solution.py:84
  139.3 6.4 %slice.109 = bf16[1,2,128,320]{2,3,1,0:T(8,128)(2,1)} slice(bf16[1,5,257,320]{2,3,1,0:T(8,128)(2,1)S(1)} %pad.58), slice={[0:1:1], [1:5:2], [2:257:2], [0:320:1]} | slice | bytes 327680 | tf_op jit(solution)/shard_map/slice | solution.py:84
  145.7 6.4 %slice.110 = bf16[1,2,128,320]{2,3,1,0:T(8,128)(2,1)} slice(bf16[1,5,257,320]{2,3,1,0:T(8,128)(2,1)S(1)} %pad.58), slice={[0:1:1], [2:5:2], [0:256:2], [0:320:1]} | slice | bytes 327680 | tf_op jit(solution)/shard_map/slice | solution.py:84
  152.2 6.4 %slice.111 = bf16[1,2,128,320]{2,3,1,0:T(8,128)(2,1)} slice(bf16[1,5,257,320]{2,3,1,0:T(8,128)(2,1)S(1)} %pad.58), slice={[0:1:1], [2:5:2], [1:257:2], [0:320:1]} | slice | bytes 327680 | tf_op jit(solution)/shard_map/slice | solution.py:84
  158.6 6.5 %slice.112 = bf16[1,2,128,320]{2,3,1,0:T(8,128)(2,1)} slice(bf16[1,5,257,320]{2,3,1,0:T(8,128)(2,1)S(1)} %pad.58), slice={[0:1:1], [2:5:2], [2:257:2], [0:320:1]} | slice | bytes 327680 | tf_op jit(solution)/shard_map/slice | solution.py:84
  174.2 4.7 %concatenate.21 = f32[2880,320]{0,1:T(8,128)} concatenate(f32[320,320]{0,1:T(8,128)S(1)} %convolution_bitcast_fusion.8, f32[320,320]{0,1:T(8,128)S(1)} %convolution_bitcast_fusion.7, f32[320,320]{0,1:T(8,128)S(1)} %convolution_bitcast_fusion.6, f32[320,320]{0,1:T(8,128)} %convolution_bitcast_fusion.5, f32[320,320]{0,1:T(8,128)} %convolution_bitcast_fusion.4, ...), dimensions={0} | concatenate | bytes 7372800 | tf_op jit(solution)/shard_map/concatenate | solution.py:90
  178.9 4.1 %broadcast_multiply_fusion = f32[2880,320]{0,1:T(8,128)} fusion(f32[2880,320]{0,1:T(8,128)} %concatenate.21), kind=kLoop, calls=%fused_computation.8 | loop fusion | flops 921600 | bytes 7372800 | tf_op jit(solution)/shard_map/mul | solution.py:90
  183.0 5.4 %copy.47 = f32[2880,320]{1,0:T(8,128)} copy(f32[2880,320]{0,1:T(8,128)} %broadcast_multiply_fusion) | data formatting | bytes 7372800
  188.6 2.6 copy.34
  191.2 11.1 %all-reduce.14 = (f32[1,320]{1,0:T(1,128)S(1)}, f32[1,320]{1,0:T(1,128)S(1)}) all-reduce(f32[1,320]{1,0:T(1,128)S(1)} %reduce_sum.93, f32[1,320]{1,0:T(1,128)S(1)} %reduce_sum.96), channel_id=1, replica_groups=mesh['groups'=2,'fsdp'=4,'rep'=4] {'fsdp'}, use_global_device_ids=true, to_apply=%region_7.8 | all-reduce | flops 640 | bytes 5120 | tf_op jit(solution)/shard_map/psum | solution.py:95
  203.1 6.1 %psum.47 = bf16[2,320]{1,0:T(2,128)(2,1)S(1)} all-reduce(bf16[2,320]{1,0:T(2,128)(2,1)S(1)} %fusion.51), channel_id=1, replica_groups=mesh['groups'=2,'fsdp'=4,'rep'=4] {'rep'}, use_global_device_ids=true, to_apply=%region_14.15 | all-reduce | flops 640 | bytes 2560 | tf_op jit(solution)/shard_map/psum | solution.py:109
  209.8 2.7 fusion.21
  216.7 52.2 %reduce-scatter.4.cloned.1.call-done = f32[720,320]{1,0:T(8,128)} async-done(((f32[2880,320]{1,0:T(8,128)}), f32[720,320]{1,0:T(8,128)}) %reduce-scatter.4.cloned.1.call-update) | async-done | bytes 921616
  268.9 2.2 copy.48
  272.2 33.2 %all-reduce.18.cloned.1.call-done = bf16[720,320]{0,1:T(8,128)(2,1)} async-done(((bf16[720,320]{0,1:T(8,128)(2,1)}), bf16[720,320]{0,1:T(8,128)(2,1)}) %all-reduce.18.cloned.1.call-update) | async-done | bytes 460816 | tf_op jit(solution)/shard_map/psum | solution.py:108
  305.4 2.0 convert_element_type.53
  (113 shorter events, 38.4 us)
Async XLA Ops:
  7.2 55.7 %copy-start = (bf16[1,2,128,320]{2,3,1,0:T(8,128)(2,1)S(1)}, bf16[1,2,128,320]{2,3,1,0:T(8,128)(2,1)}, u32[]{:S(2)}) copy-start(bf16[1,2,128,320]{2,3,1,0:T(8,128)(2,1)} %param.7) | copy-start | bytes 491524
  7.2 261.7 %reduce-scatter.4.cloned.1.call-start = ((), (), s32[]{:S(2)}) async-start(), calls=%async_computation.2 | async-start | bytes 5529600
  7.2 16.5 %collective-permute-start.1 = (bf16[720,320]{0,1:T(8,128)(2,1)}, bf16[720,320]{0,1:T(8,128)(2,1)S(1)}, u32[]{:S(2)}, u32[]{:S(2)}) collective-permute-start(bf16[720,320]{0,1:T(8,128)(2,1)} %param.6), channel_id=1, source_target_pairs={{0,4},{4,8},{8,12},{12,0},{1,5},{5,9},{9,13},{13,1},{2,6},{6,10},{... | collective-permute-start | bytes 1382408 | tf_op jit(solution)/shard_map/ppermute | solution.py:41
  23.8 14.2 %collective-permute-start.2 = (bf16[720,320]{0,1:T(8,128)(2,1)S(1)}, bf16[720,320]{0,1:T(8,128)(2,1)S(1)}, u32[]{:S(2)}, u32[]{:S(2)}) collective-permute-start(bf16[720,320]{0,1:T(8,128)(2,1)S(1)} %collective-permute-done.1), channel_id=1, source_target_pairs={{0,4},{4,8},{8,12},{12,0},{1,5},{5,9},{9,13},{13,1},{2,6},{6,10},{... | collective-permute-start | bytes 1382408 | tf_op jit(solution)/shard_map/ppermute | solution.py:41
  38.0 15.9 %collective-permute-start.3 = (bf16[720,320]{0,1:T(8,128)(2,1)S(1)}, bf16[720,320]{0,1:T(8,128)(2,1)S(1)}, u32[]{:S(2)}, u32[]{:S(2)}) collective-permute-start(bf16[720,320]{0,1:T(8,128)(2,1)S(1)} %collective-permute-done.2), channel_id=1, source_target_pairs={{0,4},{4,8},{8,12},{12,0},{1,5},{5,9},{9,13},{13,1},{2,6},{6,10},{... | collective-permute-start | bytes 1382408 | tf_op jit(solution)/shard_map/ppermute | solution.py:41
  67.9 1.5 copy-start.7
  67.9 1.7 copy-start.6
  78.1 1.4 copy-start.1
  82.0 8.3 %copy-start.15 = (f32[1,32]{1,0:T(1,128)S(1)}, f32[1,32]{1,0:T(1,128)}, u32[]{:S(2)}) copy-start(f32[1,32]{1,0:T(1,128)} %get-tuple-element.22) | copy-start | bytes 388
  82.0 8.3 %copy-start.16 = (f32[1,32]{1,0:T(1,128)S(1)}, f32[1,32]{1,0:T(1,128)}, u32[]{:S(2)}) copy-start(f32[1,32]{1,0:T(1,128)} %get-tuple-element.23) | copy-start | bytes 388
  82.0 8.7 %copy-start.14 = (f32[2,320]{1,0:T(2,128)S(1)}, f32[2,320]{1,0:T(2,128)}, u32[]{:S(2)}) copy-start(f32[2,320]{1,0:T(2,128)} %param.5) | copy-start | bytes 7684
  82.0 14.2 %copy-start.2 = (bf16[1,4,256,320]{2,3,1,0:T(8,128)(2,1)S(1)}, bf16[1,4,256,320]{2,3,1,0:T(8,128)(2,1)}, u32[]{:S(2)}) copy-start(bf16[1,4,256,320]{2,3,1,0:T(8,128)(2,1)} %param.4) | copy-start | bytes 1966084
  88.9 7.2 %collective-permute-start.4 = (bf16[1,1,256,320]{2,3,1,0:T(8,128)(2,1)S(1)}, bf16[1,1,256,320]{2,3,1,0:T(8,128)(2,1)S(1)}, u32[]{:S(2)}, u32[]{:S(2)}) collective-permute-start(bf16[1,1,256,320]{2,3,1,0:T(8,128)(2,1)S(1)} %slice.143), channel_id=1, source_target_pairs={{4,0},{8,4},{12,8},{5,1},{9,5},{13,9},{6,2},{10,6},{14,10},{7,3},{... | collective-permute-start | bytes 491528 | tf_op jit(solution)/shard_map/ppermute | solution.py:12
  99.8 6.5 %collective-permute-start = (bf16[1,1,256,320]{2,3,1,0:T(8,128)(2,1)S(1)}, bf16[1,1,256,320]{2,3,1,0:T(8,128)(2,1)S(1)}, u32[]{:S(2)}, u32[]{:S(2)}) collective-permute-start(bf16[1,1,256,320]{2,3,1,0:T(8,128)(2,1)S(1)} %slice.115), channel_id=1, source_target_pairs={{0,4},{4,8},{8,12},{1,5},{5,9},{9,13},{2,6},{6,10},{10,14},{3,7},{... | collective-permute-start | bytes 491528 | tf_op jit(solution)/shard_map/ppermute | solution.py:12
  165.1 2.7 copy-start.13
  166.3 2.6 copy-start.12
  166.6 3.4 %copy-start.11 = (bf16[1,2,128,320]{2,3,1,0:T(8,128)(2,1)S(1)}, bf16[1,2,128,320]{2,3,1,0:T(8,128)(2,1)}, u32[]{:S(2)}) copy-start(bf16[1,2,128,320]{2,3,1,0:T(8,128)(2,1)} %slice.109) | copy-start | bytes 491524
  167.8 3.2 %copy-start.10 = (bf16[1,2,128,320]{2,3,1,0:T(8,128)(2,1)S(1)}, bf16[1,2,128,320]{2,3,1,0:T(8,128)(2,1)}, u32[]{:S(2)}) copy-start(bf16[1,2,128,320]{2,3,1,0:T(8,128)(2,1)} %slice.110) | copy-start | bytes 491524
  168.9 3.2 %copy-start.9 = (bf16[1,2,128,320]{2,3,1,0:T(8,128)(2,1)S(1)}, bf16[1,2,128,320]{2,3,1,0:T(8,128)(2,1)}, u32[]{:S(2)}) copy-start(bf16[1,2,128,320]{2,3,1,0:T(8,128)(2,1)} %slice.111) | copy-start | bytes 491524
  169.9 3.2 %copy-start.8 = (bf16[1,2,128,320]{2,3,1,0:T(8,128)(2,1)S(1)}, bf16[1,2,128,320]{2,3,1,0:T(8,128)(2,1)}, u32[]{:S(2)}) copy-start(bf16[1,2,128,320]{2,3,1,0:T(8,128)(2,1)} %slice.112) | copy-start | bytes 491524
  188.5 21.3 %copy-start.3 = (bf16[1,4,256,320]{2,3,1,0:T(8,128)(2,1)S(1)}, bf16[1,4,256,320]{2,3,1,0:T(8,128)(2,1)}, u32[]{:S(2)}) copy-start(bf16[1,4,256,320]{2,3,1,0:T(8,128)(2,1)} %param.4) | copy-start | bytes 1966084
  188.5 116.9 %all-reduce.18.cloned.1.call-start = ((), (), s32[]{:S(2)}) async-start(), calls=%async_computation.1 | async-start | bytes 983040 | tf_op jit(solution)/shard_map/psum | solution.py:108
  209.8 2.7 copy-start.4
  213.9 1.6 copy-start.5
  213.9 1.6 copy-start.17
Sparse Core Ops, SparseCore 0:
  188.6 80.2 reduce-scatter.3
  272.0 33.4 all-reduce.17
